TPU v7x, 32 devices: a whole 2x2x4 slice. The times are simulated.
32 devices in a mesh: grp: 2 (over x), ex: 8 (over z, y), lay: 2 (over core).
Axes of the slice: x: 2, y: 2, z: 4, core: 2. Of those that a mesh axis runs over, the one named last changes fastest.
Arguments:
- queries: bfloat16 [512, 2, 4096], P('ex', 'lay'), may hold values from -4 to 4
- basis_s: float32 [2, 64, 64], P('lay'), may hold values from -1 to 1, as said below
- basis_a: float32 [2, 64, 64], P('lay'), may hold values from -1 to 1, as said below
- eigvals: float32 [2, 64, 64], P('lay'), may hold values from 0.004 to 20, as said below
- train_grads: bfloat16 [16384, 2, 4096], P(('grp', 'ex'), 'lay'), parts along dimension 0, may hold values from -0.0625 to 0.0625
- example_ids: int32 [16, 1024], P(('grp', 'ex')), parts along dimension 0, may hold values from 0 to 1023, each once within a row
Outputs:
- scores: float32 [512, 16384], P(None, ('grp', 'ex', 'lay')), parts along dimension 1
There are 2 independent parts, one for each index of `grp`. A program takes and returns all parts, laid end to end along the dimension named above; an argument that names none is the same for every part. Nothing has to cross between parts.
Inputs may be any that keep to these rules, and one draw needn't show every extreme that they name: `basis_s`: each layer's basis has orthonormal columns. `basis_a`: each layer's basis has orthonormal columns. `eigvals`: positive.
All inputs are finite; a program needn't handle non-finite values.
Results may differ from a plain program's by a relative error of at most 0.0029.
Values may be sent and summed in bfloat16 or wider, within the bound.
A program may use at most 64 MiB of HBM per device.

v0:
```python
import jax
import jax.numpy as jnp
from jax import lax
from jax.sharding import PartitionSpec as P

damp_ratio = 0.1


def precondition(grads, basis_s, basis_a, eigvals):
    number_rows = grads.shape[0]
    layer_count = grads.shape[1]
    rank = basis_s.shape[-1]
    highest = lax.Precision.HIGHEST
    expanded = grads.astype(jnp.float32).reshape(number_rows, layer_count, rank, rank)
    half_turn = jnp.einsum("nlik,lkm->nlim", expanded, basis_a, precision=highest)
    rotated = jnp.einsum("lij,nlim->nljm", basis_s, half_turn, precision=highest)
    damping = damp_ratio * jnp.mean(eigvals, axis=(1, 2), keepdims=True)
    scaled = rotated / (eigvals + damping)[None]
    turned_back = jnp.einsum("nljm,lpm->nljp", scaled, basis_a, precision=highest)
    restored = jnp.einsum("lij,nljp->nlip", basis_s, turned_back, precision=highest)
    return restored.reshape(number_rows, layer_count, rank * rank).astype(jnp.bfloat16)


def shards(queries, basis_s, basis_a, eigvals, train_grads, example_ids):
    stored = train_grads.reshape(train_grads.shape[0], -1)
    own_rows = precondition(queries, basis_s, basis_a, eigvals)
    query_rows = lax.all_gather(own_rows, "ex", axis=0, tiled=True)
    flattened = query_rows.reshape(query_rows.shape[0], -1)
    partial_value = lax.dot_general(
        flattened, stored, (((1,), (1,)), ((), ())), preferred_element_type=jnp.float32
    )
    ordered = jnp.take(partial_value, example_ids[0], axis=1)
    return lax.psum_scatter(ordered, "lay", scatter_dimension=1, tiled=True)


def solution(mesh):
    return jax.shard_map(
        shards,
        mesh=mesh,
        in_specs=(
            P("ex", "lay", None),
            P("lay", None, None),
            P("lay", None, None),
            P("lay", None, None),
            P(("grp", "ex"), "lay", None),
            P(("grp", "ex"), None),
        ),
        out_specs=P(None, ("grp", "ex", "lay")),
        check_vma=False,
    )
```

profile of v0, /device:TPU:1, one launch (start us, length us, event | category | flops | bytes accessed | tf_op | source)
XLA Modules:
  0.0 132.3 jit_solution(10751915736123433550)
XLA Ops:
  6.5 0.0 copy-start
  6.5 0.0 copy-start.1
  6.5 0.0 all-gather.2.cloned.1.call-start
  6.5 2.1 %reshape.90 = bf16[64,64,64]{2,1,0:T(8,128)(2,1)S(1)} reshape(bf16[64,1,4096]{2,0,1:T(8,128)(2,1)} %param.6) | data formatting | bytes 1048576 | tf_op jit(solution)/shard_map/reshape.2
  8.6 1.4 %reduce_sum.9 = f32[]{:T(128)} reduce(f32[1,64,64]{2,1,0:T(8,128)} %param.9, f32[]{:T(128)} %constant.21.clone.1), dimensions={0,1,2}, to_apply=%region_0.0 | reduce | flops 4095 | bytes 16392 | tf_op jit(solution)/shard_map/reduce_sum | solution.py:17
  10.7 0.8 add_bitcast_fusion
  11.4 0.1 copy.12
  11.5 0.0 copy-done
  11.5 3.1 %fusion.11 = f32[64,64,64]{2,0,1:T(8,128)S(1)} fusion(bf16[64,64,64]{2,1,0:T(8,128)(2,1)S(1)} %reshape.90, f32[1,64,64]{2,1,0:T(8,128)S(1)} %copy-done), kind=kOutput, calls=%fused_computation.14 | convolution fusion | flops 201326592 | bytes 1589248 | tf_op jit(solution)/shard_map/nlik,lkm->nlim/dot_general | solution.py:15
  14.6 0.0 copy-done.1
  14.7 1.8 %fusion.6 = f32[64,64,64]{2,1,0:T(8,128)S(1)} fusion(f32[64,64,64]{2,0,1:T(8,128)S(1)} %fusion.11, f32[1,64,64]{2,1,0:T(8,128)S(1)} %copy-done.1), kind=kOutput, calls=%fused_computation.7 | convolution fusion | flops 201326592 | bytes 2113536 | tf_op jit(solution)/shard_map/lij,nlim->nljm/dot_general | solution.py:16
  16.5 2.1 %fusion.4 = f32[64,64,64]{1,2,0:T(8,128)S(1)} fusion(f32[64,64,64]{2,1,0:T(8,128)S(1)} %fusion.6, f32[64,64]{0,1:T(8,128)S(1)} %copy.12, f32[1,64,64]{2,1,0:T(8,128)S(1)} %copy-done), kind=kOutput, calls=%fused_computation.6 | convolution fusion | flops 201588736 | bytes 2129920 | tf_op jit(solution)/shard_map/nljm,lpm->nljp/dot_general | solution.py:19
  18.6 1.8 %fusion.8 = bf16[64,1,64,64]{2,3,0,1:T(8,128)(2,1)S(1)} fusion(f32[64,64,64]{1,2,0:T(8,128)S(1)} %fusion.4, f32[1,64,64]{2,1,0:T(8,128)S(1)} %copy-done.1), kind=kOutput, calls=%fused_computation.11 | convolution fusion | flops 201588736 | bytes 1589248 | tf_op jit(solution)/shard_map/lij,nljp->nlip/dot_general | solution.py:20
  20.4 0.0 copy-start.2
  20.4 0.7 copy.13
  21.1 1.6 %convert_element_type.24 = bf16[64,1,4096]{2,0,1:T(8,128)(2,1)} reshape(bf16[64,1,64,64]{3,2,0,1:T(8,128)(2,1)S(1)} %copy.13) | data formatting | bytes 1048576 | tf_op jit(solution)/shard_map/convert_element_type | solution.py:21
  22.7 0.0 all-gather.2.cloned.1.call-update
  22.7 0.2 reduce-scatter.2.cloned.1.call-start
  23.0 0.0 copy-done.2
  23.0 73.5 %all-gather.2.cloned.1.call-done = bf16[512,1,4096]{2,0,1:T(8,128)(2,1)} async-done(((bf16[64,1,4096]{2,0,1:T(8,128)(2,1)}), bf16[512,1,4096]{2,0,1:T(8,128)(2,1)}) %all-gather.2.cloned.1.call-update) | async-done | bytes 4194320 | tf_op jit(solution)/shard_map/all_gather | solution.py:27
  96.5 8.2 %fusion = f32[512,1024]{0,1:T(8,128)S(1)} fusion(bf16[1024,1,4096]{2,0,1:T(8,128)(2,1)} %param.10, bf16[512,1,4096]{2,0,1:T(8,128)(2,1)} %all-gather.2.cloned.1.call-done), kind=kOutput, calls=%fused_computation.1 | convolution fusion | flops 4294967296 | bytes 14680064 | tf_op jit(solution)/shard_map/dot_general | solution.py:29
  104.8 4.9 %gather_fusion = f32[1024,512]{1,0:T(8,128)} fusion(f32[512,1024]{0,1:T(8,128)S(1)} %fusion, s32[1024]{0:T(1024)S(1)} %broadcast_clamp_fusion), kind=kCustom, calls=%fused_computation | custom fusion | bytes 4198400 | tf_op jit(solution)/shard_map/jit(_take)/gather | solution.py:32
  109.6 3.1 %select_bitcast_fusion = f32[512,1024]{0,1:T(8,128)} fusion(f32[1024,512]{1,0:T(8,128)} %gather_fusion, pred[1024]{0:T(1024)(128)(4,1)S(1)} %compare_and_fusion), kind=kLoop, calls=%fused_computation.9 | loop fusion | flops 524288 | bytes 4195328 | tf_op jit(solution)/shard_map/jit(_take)/select_n | solution.py:32
  112.8 0.0 reduce-scatter.2.cloned.1.call-update
  112.8 10.1 %reduce-scatter.2.cloned.1.call-done = f32[512,512]{0,1:T(8,128)} async-done(((f32[512,1024]{0,1:T(8,128)}), f32[512,512]{0,1:T(8,128)}) %reduce-scatter.2.cloned.1.call-update) | async-done | bytes 1048592 | tf_op jit(solution)/shard_map/reduce_scatter | solution.py:33
  122.9 2.5 %copy.15 = f32[512,512]{1,0:T(8,128)} copy(f32[512,512]{0,1:T(8,128)} %reduce-scatter.2.cloned.1.call-done) | data formatting | bytes 2097152 | tf_op jit(solution)/shard_map/reduce_scatter | solution.py:33
  (3 shorter events, 0.0 us)
Async XLA Ops:
  6.5 5.0 %copy-start = (f32[1,64,64]{2,1,0:T(8,128)S(1)}, f32[1,64,64]{2,1,0:T(8,128)}, u32[]{:S(2)}) copy-start(f32[1,64,64]{2,1,0:T(8,128)} %param.8) | copy-start | bytes 49156
  6.5 8.1 %copy-start.1 = (f32[1,64,64]{2,1,0:T(8,128)S(1)}, f32[1,64,64]{2,1,0:T(8,128)}, u32[]{:S(2)}) copy-start(f32[1,64,64]{2,1,0:T(8,128)} %param.7) | copy-start | bytes 49156
  6.5 90.0 %all-gather.2.cloned.1.call-start = ((), (), s32[]{:S(2)}) async-start(), calls=%async_computation.1 | async-start | bytes 4718592 | tf_op jit(solution)/shard_map/all_gather | solution.py:27
  20.4 2.5 %copy-start.2 = (s32[1,1024]{1,0:T(1,128)S(1)}, s32[1,1024]{1,0:T(1,128)}, u32[]{:S(2)}) copy-start(s32[1,1024]{1,0:T(1,128)} %param.11) | copy-start | bytes 12292
  22.7 100.2 %reduce-scatter.2.cloned.1.call-start = ((), (), s32[]{:S(2)}) async-start(), calls=%async_computation.2 | async-start | bytes 3145728 | tf_op jit(solution)/shard_map/reduce_scatter | solution.py:33
Sparse Core Ops, SparseCore 0:
  22.9 73.6 all-gather.1
  112.9 9.9 reduce-scatter.1
where the time goes:
time: 133 us; the launch traced here: 132 us
  waiting for transfers between devices  83.7 us (63%)
  matrix products  17.1 us (13%)
  between operations  14.2 us (11%)
  local copies, waits for them, and re-layouts  11.8 us (9%)
  other arithmetic  5.3 us (4%)
    all_gather x1, waiting for transfers between devices, shards(): query_rows = lax.all_gather(own_rows, 'ex', axis=0, tiled=True)  73.5 us
    reduce_scatter x1, waiting for transfers between devices, shards(): return lax.psum_scatter(ordered, 'lay', scatter_dimension=1, tiled=True)  10.1 us
    dot_general x1, matrix products, shards(): lax.dot_general(flattened, stored, (((1,), (1,)), ((), ())), preferred_el...  8.22 us
    gather x1, local copies, waits for them, and re-layouts, shards(): ordered = jnp.take(partial_value, example_ids[0], axis=1)  4.87 us
    select_n x2, other arithmetic, shards(): ordered = jnp.take(partial_value, example_ids[0], axis=1)  3.15 us
    dot_general x1, matrix products, precondition(): jnp.einsum('nlik,lkm->nlim', expanded, basis_a, precision=highest)  3.14 us
  transfers between devices with their start and end apart: 2, of which 2 were waited for; matrix products, arithmetic and copies ran while one was open for 0% of the time, Pallas kernels for 0%

commit v1 on v0

--- a/solution.py
+++ b/solution.py
@@ -1,9 +1,15 @@
+import functools
+
 import jax
 import jax.numpy as jnp
 from jax import lax
+from jax.experimental import pallas as pl
+from jax.experimental.pallas import tpu as pltpu
 from jax.sharding import PartitionSpec as P
 
 damp_ratio = 0.1
+pairs = 4
+MESH = pl.DeviceIdType.MESH
 
 
 def precondition(grads, basis_s, basis_a, eigvals):
@@ -21,21 +27,273 @@
     return restored.reshape(number_rows, layer_count, rank * rank).astype(jnp.bfloat16)
 
 
-def shards(queries, basis_s, basis_a, eigvals, train_grads, example_ids):
+def score_kernel(
+    line, own_ref, ids_ref, train_ref, out_ref,
+    stored, hot, perm, held, acc, arrived,
+    load_sem, own_sem, z_recv, zr_send, zl_send, y_recv, y_send, x_recv, x_send, c_recv, c_send,
+):
+    grp = lax.axis_index("grp")
+    ex = lax.axis_index("ex")
+    core = lax.axis_index("lay")
+    zz = ex // 2
+    w = ex % 2
+    side = grp % 2
+    rows = own_ref.shape[2]
+    examples = train_ref.shape[0]
+    chunk = own_ref.shape[3]
+    half = examples // 2
+    right = {"ex": lax.rem(ex + 2, 2 * line)}
+    left = {"ex": lax.rem(ex + 2 * line - 2, 2 * line)}
+    across_y = {"ex": zz * 2 + (1 - w)}
+    across_x = {"grp": (grp // 2) * 2 + (1 - side)}
+    across_c = {"lay": 1 - core}
+    has_left = zz > 0
+    has_right = zz < line - 1
+
+    def load(p):
+        return pltpu.make_async_copy(
+            train_ref.at[:, pl.ds(p * 2 * chunk, 2 * chunk)], stored.at[p], load_sem.at[p]
+        )
+
+    def z_copy(src, b, p, send, target):
+        return pltpu.make_async_remote_copy(
+            src_ref=src, dst_ref=held.at[b, p, :, w], send_sem=send.at[b, p],
+            recv_sem=z_recv.at[b, p], device_id=target, device_id_type=MESH,
+        )
+
+    def own_z(p, send, target):
+        return z_copy(own_ref.at[p], zz, p, send, target)
+
+    def pass_z(b, p, send, target):
+        return z_copy(held.at[b, p, :, w], b, p, send, target)
+
+    def y_copy(src, b, p):
+        return pltpu.make_async_remote_copy(
+            src_ref=src, dst_ref=held.at[b, p, side, w], send_sem=y_send.at[b, p],
+            recv_sem=y_recv.at[b, p], device_id=across_y, device_id_type=MESH,
+        )
+
+    def y_arrival(b, p):
+        slot = held.at[b, p, side, 1 - w]
+        return pltpu.make_async_remote_copy(
+            src_ref=slot, dst_ref=slot, send_sem=y_send.at[b, p],
+            recv_sem=y_recv.at[b, p], device_id=across_y, device_id_type=MESH,
+        )
+
+    def x_copy(b, p, which):
+        slot = held.at[b, p, which, 1 - w]
+        return pltpu.make_async_remote_copy(
+            src_ref=slot, dst_ref=slot, send_sem=x_send.at[b, p],
+            recv_sem=x_recv.at[b, p], device_id=across_x, device_id_type=MESH,
+        )
+
+    def c_copy(b):
+        return pltpu.make_async_remote_copy(
+            src_ref=acc.at[b, 1 - core], dst_ref=arrived.at[b], send_sem=c_send.at[b],
+            recv_sem=c_recv.at[b], device_id=across_c, device_id_type=MESH,
+        )
+
+    @pl.loop(0, pairs)
+    def _(p):
+        load(p).start()
+
+    barrier = pltpu.get_barrier_semaphore()
+
+    @pl.when(has_left)
+    def _():
+        pl.semaphore_signal(barrier, inc=1, device_id=left, device_id_type=MESH)
+
+    @pl.when(has_right)
+    def _():
+        pl.semaphore_signal(barrier, inc=1, device_id=right, device_id_type=MESH)
+
+    for target in (across_y, across_x, across_c):
+        pl.semaphore_signal(barrier, inc=1, device_id=target, device_id_type=MESH)
+    pl.semaphore_wait(barrier, 3 + has_left.astype(jnp.int32) + has_right.astype(jnp.int32))
+
+    @pl.loop(0, pairs)
+    def _(p):
+        @pl.when(has_right)
+        def _():
+            own_z(p, zr_send, right).start()
+
+        @pl.when(has_left)
+        def _():
+            own_z(p, zl_send, left).start()
+
+        y_copy(own_ref.at[p, side], zz, p).start()
+
+    @pl.loop(0, pairs)
+    def _(p):
+        pltpu.make_async_copy(own_ref.at[p], held.at[zz, p, :, w], own_sem.at[p]).start()
+
+    spread = jnp.broadcast_to(ids_ref[...].astype(jnp.float32), (128, examples)).T
+    lanes = lax.broadcasted_iota(jnp.int32, (examples, 128), 1).astype(jnp.float32)
+    for tile in range(examples // 128):
+        hot[:, tile * 128:(tile + 1) * 128] = jnp.where(
+            spread == lanes + float(tile * 128), 1.0, 0.0
+        ).astype(jnp.bfloat16)
+
+    @pl.loop(0, pairs)
+    def _(p):
+        pltpu.make_async_copy(own_ref.at[p], held.at[zz, p, :, w], own_sem.at[p]).wait()
+
+    def both(s, act):
+        t = s // pairs
+        p = s % pairs
+        valid = jnp.logical_and(s >= 0, t < line)
+
+        @pl.when(jnp.logical_and(valid, zz - t >= 0))
+        def _():
+            act(zz - t, t, p, True)
+
+        @pl.when(jnp.logical_and(jnp.logical_and(valid, t > 0), zz + t < line))
+        def _():
+            act(zz + t, t, p, False)
+
+    def relay_z(b, t, p, from_left):
+        @pl.when(t > 0)
+        def _():
+            if from_left:
+                pass_z(b, p, zr_send, left).wait_recv()
+
+                @pl.when(has_right)
+                def _():
+                    pass_z(b, p, zr_send, right).start()
+            else:
+                pass_z(b, p, zl_send, right).wait_recv()
+
+                @pl.when(has_left)
+                def _():
+                    pass_z(b, p, zl_send, left).start()
+
+            y_copy(held.at[b, p, side, w], b, p).start()
+
+    def relay_x(b, t, p, from_left):
+        y_arrival(b, p).wait_recv()
+        x_copy(b, p, side).start()
+
+    def multiply(b, t, p, from_left):
+        x_copy(b, p, 1 - side).wait_recv()
+        for part in range(2):
+            value = None
+            for h in range(2):
+                term = lax.dot_general(
+                    held[b, p, h].reshape(2 * rows, chunk),
+                    perm[p, h, part * half:(part + 1) * half, :],
+                    (((1,), (1,)), ((), ())), preferred_element_type=jnp.float32,
+                )
+                value = term if value is None else value + term
+
+            @pl.when(p == 0)
+            def _():
+                acc[b, part] = value
+
+            @pl.when(p > 0)
+            def _():
+                acc[b, part] = acc[b, part] + value
+
+        @pl.when(p == pairs - 1)
+        def _():
+            c_copy(b).start()
+
+    def finish(b, t, p, from_left):
+        @pl.when(p == pairs - 1)
+        def _():
+            c_copy(b).wait_recv()
+            out_ref[b] = acc[b, core] + arrived[b]
+
+    @pl.loop(0, line * pairs + 3)
+    def _(s):
+        both(s, relay_z)
+        both(s - 1, relay_x)
+
+        @pl.when(s < pairs)
+        def _():
+            load(s).wait()
+
+            @pl.loop(0, 4)
+            def _(part):
+                quarter = examples // 4
+                picked = pl.ds(part * quarter, quarter)
+                for h in range(2):
+                    perm[s, h, picked, :] = jnp.dot(
+                        hot[picked, :], stored[s, :, h * chunk:(h + 1) * chunk],
+                        preferred_element_type=jnp.float32,
+                    ).astype(jnp.bfloat16)
+
+        both(s - 2, multiply)
+        both(s - 3, finish)
+
+    @pl.loop(0, line * pairs)
+    def _(s):
+        b = s // pairs
+        p = s % pairs
+
+        @pl.when(jnp.logical_and(has_right, b <= zz))
+        def _():
+            pass_z(b, p, zr_send, right).wait_send()
+
+        @pl.when(jnp.logical_and(has_left, b >= zz))
+        def _():
+            pass_z(b, p, zl_send, left).wait_send()
+
+        y_copy(held.at[b, p, side, w], b, p).wait_send()
+        x_copy(b, p, side).wait_send()
+
+        @pl.when(p == 0)
+        def _():
+            c_copy(b).wait_send()
+
+
+def scores_of(own, ids, train, devices):
+    rows = own.shape[2]
+    chunk = own.shape[3]
+    examples = train.shape[0]
+    line = devices // 2
+    dma = pltpu.SemaphoreType.DMA
+    grid_sems = [dma((line, pairs)) for _ in range(7)]
+    return pl.pallas_call(
+        functools.partial(score_kernel, line),
+        out_shape=jax.ShapeDtypeStruct((line, 2 * rows, examples // 2), jnp.float32),
+        in_specs=[
+            pl.BlockSpec(memory_space=pltpu.VMEM),
+            pl.BlockSpec(memory_space=pltpu.VMEM),
+            pl.BlockSpec(memory_space=pl.ANY),
+        ],
+        out_specs=pl.BlockSpec(memory_space=pltpu.VMEM),
+        scratch_shapes=[
+            pltpu.VMEM((pairs, examples, 2 * chunk), jnp.bfloat16),
+            pltpu.VMEM((examples, examples), jnp.bfloat16),
+            pltpu.VMEM((pairs, 2, examples, chunk), jnp.bfloat16),
+            pltpu.VMEM((line, pairs, 2, 2, rows, chunk), jnp.bfloat16),
+            pltpu.VMEM((line, 2, 2 * rows, examples // 2), jnp.float32),
+            pltpu.VMEM((line, 2 * rows, examples // 2), jnp.float32),
+            dma((pairs,)),
+            dma((pairs,)),
+            *grid_sems,
+            dma((line,)),
+            dma((line,)),
+        ],
+        compiler_params=pltpu.CompilerParams(
+            collective_id=0, has_side_effects=True, vmem_limit_bytes=56 * 1024 * 1024
+        ),
+    )(own, ids, train)
+
+
+def shards(devices, queries, basis_s, basis_a, eigvals, train_grads, example_ids):
     stored = train_grads.reshape(train_grads.shape[0], -1)
     own_rows = precondition(queries, basis_s, basis_a, eigvals)
-    query_rows = lax.all_gather(own_rows, "ex", axis=0, tiled=True)
-    flattened = query_rows.reshape(query_rows.shape[0], -1)
-    partial_value = lax.dot_general(
-        flattened, stored, (((1,), (1,)), ((), ())), preferred_element_type=jnp.float32
-    )
-    ordered = jnp.take(partial_value, example_ids[0], axis=1)
-    return lax.psum_scatter(ordered, "lay", scatter_dimension=1, tiled=True)
+    rows = own_rows.shape[0]
+    cut = own_rows.reshape(rows, 2 * pairs, -1).transpose(1, 0, 2)
+    cut = cut.reshape(pairs, 2, rows, cut.shape[-1])
+    scores = scores_of(cut, example_ids, stored, devices)
+    return scores.reshape(devices * rows, -1)
 
 
 def solution(mesh):
     return jax.shard_map(
-        shards,
+        functools.partial(shards, mesh.shape["ex"]),
         mesh=mesh,
         in_specs=(
             P("ex", "lay", None),

time: 133 us -> 78.2 us (0.59)
  waiting for transfers between devices: 83.7 us -> 0 us
  Pallas kernels: 0 us -> 59.5 us
  between operations: 14.2 us -> 0.73 us
  matrix products: 17.1 us -> 8.89 us
  local copies, waits for them, and re-layouts: 11.8 us -> 6.63 us
  other arithmetic: 5.3 us -> 2.14 us
    all_gather x1 -> x0, waiting for transfers between devices: 73.5 us -> none  [shards(): query_rows = lax.all_gather(own_rows, 'ex', axis=0, tiled=True)]
    pallas_call x0 -> x1, Pallas kernels: none -> 59.5 us  [scores_of(): pl.pallas_call(functools.partial(score_kernel, line), out_shape=jax.Shape...]
    reduce_scatter x1 -> x0, waiting for transfers between devices: 10.1 us -> none  [shards(): return lax.psum_scatter(ordered, 'lay', scatter_dimension=1, tiled=True)]
    dot_general x1 -> x0, matrix products: 8.22 us -> none  [shards(): lax.dot_general(flattened, stored, (((1,), (1,)), ((), ())), preferred_el...]
    gather x1 -> x0, local copies, waits for them, and re-layouts: 4.87 us -> none  [shards(): ordered = jnp.take(partial_value, example_ids[0], axis=1)]
    select_n x2 -> x0, other arithmetic: 3.15 us -> none  [shards(): ordered = jnp.take(partial_value, example_ids[0], axis=1)]
    reduce_scatter x1 -> x0, local copies, waits for them, and re-layouts: 2.53 us -> none  [shards(): return lax.psum_scatter(ordered, 'lay', scatter_dimension=1, tiled=True)]
    unnamed x6 -> x5, local copies, waits for them, and re-layouts: 0.01 us -> 2.27 us
  transfers between devices with their start and end apart: 2 -> 0, of which waited for: 2 -> 0; matrix products, arithmetic and copies ran while one was open for 0% -> 0% of each run, Pallas kernels for 0% -> 0%
where the time goes in v1:
time: 78.2 us; the launch traced here: 77.9 us
  Pallas kernels  59.5 us (76%)
  matrix products  8.89 us (11%)
  local copies, waits for them, and re-layouts  6.63 us (8%)
  other arithmetic  2.14 us (3%)
    pallas_call x1, Pallas kernels, scores_of(): pl.pallas_call(functools.partial(score_kernel, line), out_shape=jax.Shape...  59.5 us
    dot_general x1, matrix products, precondition(): jnp.einsum('nlik,lkm->nlim', expanded, basis_a, precision=highest)  3.14 us
    unnamed x5, local copies, waits for them, and re-layouts  2.27 us
    dot_general x1, matrix products, precondition(): jnp.einsum('nljm,lpm->nljp', scaled, basis_a, precision=highest)  2.12 us
    another operation x1, local copies, waits for them, and re-layouts  2.07 us
    dot_general x1, matrix products, precondition(): jnp.einsum('lij,nlim->nljm', basis_s, half_turn, precision=highest)  1.84 us
    dot_general x1, matrix products, precondition(): jnp.einsum('lij,nljp->nlip', basis_s, turned_back, precision=highest)  1.78 us

profile of v1, /device:TPU:1, one launch (start us, length us, event | category | flops | bytes accessed | tf_op | source)
XLA Modules:
  0.0 77.9 jit_solution(1028258926485953199)
XLA Ops:
  0.0 0.0 copy-start
  0.0 1.4 %reduce_sum.9 = f32[]{:T(128)} reduce(f32[1,64,64]{2,1,0:T(8,128)} %param.9, f32[]{:T(128)} %constant.6.clone.1), dimensions={0,1,2}, to_apply=%region_0.0 | reduce | flops 4095 | bytes 16392 | tf_op jit(solution)/shard_map/reduce_sum | solution.py:23
  2.0 0.8 add_bitcast_fusion
  2.8 0.1 copy.10
  2.9 0.0 copy-start.1
  2.9 2.1 %reshape.52 = bf16[64,64,64]{2,1,0:T(8,128)(2,1)S(1)} reshape(bf16[64,1,4096]{2,0,1:T(8,128)(2,1)} %param.6) | data formatting | bytes 1048576 | tf_op jit(solution)/shard_map/reshape.1
  5.0 0.0 copy-done
  5.0 3.1 %fusion.8 = f32[64,64,64]{2,0,1:T(8,128)S(1)} fusion(bf16[64,64,64]{2,1,0:T(8,128)(2,1)S(1)} %reshape.52, f32[1,64,64]{2,1,0:T(8,128)S(1)} %copy-done), kind=kOutput, calls=%fused_computation.9 | convolution fusion | flops 201326592 | bytes 1589248 | tf_op jit(solution)/shard_map/nlik,lkm->nlim/dot_general | solution.py:21
  8.1 0.0 copy-done.1
  8.1 1.8 %fusion.3 = f32[64,64,64]{2,1,0:T(8,128)S(1)} fusion(f32[64,64,64]{2,0,1:T(8,128)S(1)} %fusion.8, f32[1,64,64]{2,1,0:T(8,128)S(1)} %copy-done.1), kind=kOutput, calls=%fused_computation.3 | convolution fusion | flops 201326592 | bytes 2113536 | tf_op jit(solution)/shard_map/lij,nlim->nljm/dot_general | solution.py:22
  10.0 2.1 %fusion.1 = f32[64,64,64]{1,2,0:T(8,128)S(1)} fusion(f32[64,64,64]{2,1,0:T(8,128)S(1)} %fusion.3, f32[64,64]{0,1:T(8,128)S(1)} %copy.10, f32[1,64,64]{2,1,0:T(8,128)S(1)} %copy-done), kind=kOutput, calls=%fused_computation.2 | convolution fusion | flops 201588736 | bytes 2129920 | tf_op jit(solution)/shard_map/nljm,lpm->nljp/dot_general | solution.py:25
  12.1 1.8 %fusion.5 = bf16[64,1,64,64]{2,3,0,1:T(8,128)(2,1)S(1)} fusion(f32[64,64,64]{1,2,0:T(8,128)S(1)} %fusion.1, f32[1,64,64]{2,1,0:T(8,128)S(1)} %copy-done.1), kind=kOutput, calls=%fused_computation.6 | convolution fusion | flops 201588736 | bytes 1589248 | tf_op jit(solution)/shard_map/lij,nljp->nlip/dot_general | solution.py:26
  13.9 0.7 copy.11
  14.6 0.6 convert_element_type.19
  15.2 0.9 %copy.12 = bf16[8,64,512]{2,1,0:T(8,128)(2,1)} copy(bf16[8,64,512]{2,0,1:T(8,128)(2,1)S(1)} %bitcast.51) | data formatting | bytes 1048576 | tf_op jit(solution)/shard_map/transpose | solution.py:288
  16.1 59.5 %shard_map.64 = f32[4,128,512]{2,1,0:T(8,128)} custom-call(bf16[4,2,64,512]{3,2,1,0:T(8,128)(2,1)} %bitcast.52, s32[1,1024]{1,0:T(1,128)} %ids_ref.1, bf16[1024,4096]{1,0:T(8,128)(2,1)} %bitcast.49), custom_call_target="tpu_custom_call" | custom-call | tf_op jit(solution)/shard_map/pallas_call | solution.py:256
  75.6 2.3 %copy.16 = f32[512,512]{1,0:T(8,128)} copy(f32[512,512]{1,0:T(8,128)} %bitcast.50) | data formatting | bytes 2097152
Async XLA Ops:
  0.0 5.0 %copy-start = (f32[1,64,64]{2,1,0:T(8,128)S(1)}, f32[1,64,64]{2,1,0:T(8,128)}, u32[]{:S(2)}) copy-start(f32[1,64,64]{2,1,0:T(8,128)} %param.8) | copy-start | bytes 49156
  2.9 5.2 %copy-start.1 = (f32[1,64,64]{2,1,0:T(8,128)S(1)}, f32[1,64,64]{2,1,0:T(8,128)}, u32[]{:S(2)}) copy-start(f32[1,64,64]{2,1,0:T(8,128)} %param.7) | copy-start | bytes 49156

commit v2 on v1

--- a/solution.py
+++ b/solution.py
@@ -141,13 +141,13 @@
     def both(s, act):
         t = s // pairs
         p = s % pairs
-        valid = jnp.logical_and(s >= 0, t < line)
+        valid = jnp.logical_and(jnp.asarray(s) >= 0, jnp.asarray(t) < line)
 
         @pl.when(jnp.logical_and(valid, zz - t >= 0))
         def _():
             act(zz - t, t, p, True)
 
-        @pl.when(jnp.logical_and(jnp.logical_and(valid, t > 0), zz + t < line))
+        @pl.when(jnp.logical_and(jnp.logical_and(valid, jnp.asarray(t) > 0), zz + t < line))
         def _():
             act(zz + t, t, p, False)
 
@@ -203,10 +203,21 @@
             c_copy(b).wait_recv()
             out_ref[b] = acc[b, core] + arrived[b]
 
-    @pl.loop(0, line * pairs + 3)
+    @pl.loop(0, pairs)
+    def _(p):
+        relay_x(zz, 0, p, True)
+
+    def reached(s):
+        ready = jnp.minimum(2 * (s - pairs + 1), s + pairs - 1)
+        return jnp.minimum(jnp.maximum(ready, 0), line * pairs)
+
+    @pl.loop(0, (line + 1) * pairs)
     def _(s):
-        both(s, relay_z)
-        both(s - 1, relay_x)
+        both(s + pairs, relay_z)
+
+        @pl.when(s > 0)
+        def _():
+            both(s + pairs - 1, relay_x)
 
         @pl.when(s < pairs)
         def _():
@@ -222,8 +233,12 @@
                         preferred_element_type=jnp.float32,
                     ).astype(jnp.bfloat16)
 
-        both(s - 2, multiply)
-        both(s - 3, finish)
+        @pl.loop(reached(s - 1), reached(s))
+        def _(m):
+            both(m, multiply)
+            both(m - 1, finish)
+
+    both(line * pairs - 1, finish)
 
     @pl.loop(0, line * pairs)
     def _(s):

time: 78.2 us -> 72.6 us (0.928)
  Pallas kernels: 59.5 us -> 53.9 us
    pallas_call x1, Pallas kernels: 59.5 us -> 53.9 us  [scores_of(): pl.pallas_call(functools.partial(score_kernel, line), out_shape=jax.Shape...]
where the time goes in v2:
time: 72.6 us; the launch traced here: 72.2 us
  Pallas kernels  53.9 us (74%)
  matrix products  8.89 us (12%)
  local copies, waits for them, and re-layouts  6.63 us (9%)
  other arithmetic  2.14 us (3%)
  between operations  0.73 us (1%)
    pallas_call x1, Pallas kernels, scores_of(): pl.pallas_call(functools.partial(score_kernel, line), out_shape=jax.Shape...  53.9 us
    dot_general x1, matrix products, precondition(): jnp.einsum('nlik,lkm->nlim', expanded, basis_a, precision=highest)  3.14 us
    unnamed x5, local copies, waits for them, and re-layouts  2.27 us
    dot_general x1, matrix products, precondition(): jnp.einsum('nljm,lpm->nljp', scaled, basis_a, precision=highest)  2.12 us
    another operation x1, local copies, waits for them, and re-layouts  2.07 us
    dot_general x1, matrix products, precondition(): jnp.einsum('lij,nlim->nljm', basis_s, half_turn, precision=highest)  1.84 us
    dot_general x1, matrix products, precondition(): jnp.einsum('lij,nljp->nlip', basis_s, turned_back, precision=highest)  1.78 us

profile of v2, /device:TPU:1, one launch (start us, length us, event | category | flops | bytes accessed | tf_op | source)
XLA Modules:
  0.0 72.2 jit_solution(7094817659388309238)
XLA Ops:
  0.0 0.0 copy-start
  0.0 1.4 %reduce_sum.9 = f32[]{:T(128)} reduce(f32[1,64,64]{2,1,0:T(8,128)} %param.9, f32[]{:T(128)} %constant.6.clone.1), dimensions={0,1,2}, to_apply=%region_0.0 | reduce | flops 4095 | bytes 16392 | tf_op jit(solution)/shard_map/reduce_sum | solution.py:23
  2.0 0.8 %add_bitcast_fusion = f32[64,64]{1,0:T(8,128)S(1)} fusion(f32[1,64,64]{2,1,0:T(8,128)} %param.9, f32[]{:T(128)S(6)} %mul.4), kind=kLoop, calls=%fused_computation.13 | loop fusion | flops 4096 | bytes 32772 | tf_op jit(solution)/shard_map/div | solution.py:24
  2.8 0.1 copy.10
  2.9 0.0 copy-start.1
  2.9 2.1 %reshape.52 = bf16[64,64,64]{2,1,0:T(8,128)(2,1)S(1)} reshape(bf16[64,1,4096]{2,0,1:T(8,128)(2,1)} %param.6) | data formatting | bytes 1048576 | tf_op jit(solution)/shard_map/reshape.1
  5.0 0.0 copy-done
  5.0 3.1 %fusion.8 = f32[64,64,64]{2,0,1:T(8,128)S(1)} fusion(bf16[64,64,64]{2,1,0:T(8,128)(2,1)S(1)} %reshape.52, f32[1,64,64]{2,1,0:T(8,128)S(1)} %copy-done), kind=kOutput, calls=%fused_computation.9 | convolution fusion | flops 201326592 | bytes 1589248 | tf_op jit(solution)/shard_map/nlik,lkm->nlim/dot_general | solution.py:21
  8.1 0.0 copy-done.1
  8.1 1.8 %fusion.3 = f32[64,64,64]{2,1,0:T(8,128)S(1)} fusion(f32[64,64,64]{2,0,1:T(8,128)S(1)} %fusion.8, f32[1,64,64]{2,1,0:T(8,128)S(1)} %copy-done.1), kind=kOutput, calls=%fused_computation.3 | convolution fusion | flops 201326592 | bytes 2113536 | tf_op jit(solution)/shard_map/lij,nlim->nljm/dot_general | solution.py:22
  10.0 2.1 %fusion.1 = f32[64,64,64]{1,2,0:T(8,128)S(1)} fusion(f32[64,64,64]{2,1,0:T(8,128)S(1)} %fusion.3, f32[64,64]{0,1:T(8,128)S(1)} %copy.10, f32[1,64,64]{2,1,0:T(8,128)S(1)} %copy-done), kind=kOutput, calls=%fused_computation.2 | convolution fusion | flops 201588736 | bytes 2129920 | tf_op jit(solution)/shard_map/nljm,lpm->nljp/dot_general | solution.py:25
  12.1 1.8 %fusion.5 = bf16[64,1,64,64]{2,3,0,1:T(8,128)(2,1)S(1)} fusion(f32[64,64,64]{1,2,0:T(8,128)S(1)} %fusion.1, f32[1,64,64]{2,1,0:T(8,128)S(1)} %copy-done.1), kind=kOutput, calls=%fused_computation.6 | convolution fusion | flops 201588736 | bytes 1589248 | tf_op jit(solution)/shard_map/lij,nljp->nlip/dot_general | solution.py:26
  13.9 0.7 copy.11
  14.6 0.6 convert_element_type.19
  15.2 0.9 %copy.12 = bf16[8,64,512]{2,1,0:T(8,128)(2,1)} copy(bf16[8,64,512]{2,0,1:T(8,128)(2,1)S(1)} %bitcast.51) | data formatting | bytes 1048576 | tf_op jit(solution)/shard_map/transpose | solution.py:303
  16.1 53.9 %shard_map.64 = f32[4,128,512]{2,1,0:T(8,128)} custom-call(bf16[4,2,64,512]{3,2,1,0:T(8,128)(2,1)} %bitcast.52, s32[1,1024]{1,0:T(1,128)} %ids_ref.1, bf16[1024,4096]{1,0:T(8,128)(2,1)} %bitcast.49), custom_call_target="tpu_custom_call" | custom-call | tf_op jit(solution)/shard_map/pallas_call | solution.py:271
  70.0 2.3 %copy.16 = f32[512,512]{1,0:T(8,128)} copy(f32[512,512]{1,0:T(8,128)} %bitcast.50) | data formatting | bytes 2097152
Async XLA Ops:
  0.0 5.0 %copy-start = (f32[1,64,64]{2,1,0:T(8,128)S(1)}, f32[1,64,64]{2,1,0:T(8,128)}, u32[]{:S(2)}) copy-start(f32[1,64,64]{2,1,0:T(8,128)} %param.8) | copy-start | bytes 49156
  2.9 5.2 %copy-start.1 = (f32[1,64,64]{2,1,0:T(8,128)S(1)}, f32[1,64,64]{2,1,0:T(8,128)}, u32[]{:S(2)}) copy-start(f32[1,64,64]{2,1,0:T(8,128)} %param.7) | copy-start | bytes 49156

commit v3 on v2

--- a/solution.py
+++ b/solution.py
@@ -9,6 +9,7 @@
 
 damp_ratio = 0.1
 pairs = 4
+shared = 2
 MESH = pl.DeviceIdType.MESH
 
 
@@ -30,7 +31,8 @@
 def score_kernel(
     line, own_ref, ids_ref, train_ref, out_ref,
     stored, hot, perm, held, acc, arrived,
-    load_sem, own_sem, z_recv, zr_send, zl_send, y_recv, y_send, x_recv, x_send, c_recv, c_send,
+    load_sem, own_sem, z_recv, zr_send, zl_send, y_recv, y_send, x_recv, x_send, twin_recv, twin_send,
+    c_recv, c_send,
 ):
     grp = lax.axis_index("grp")
     ex = lax.axis_index("ex")
@@ -55,23 +57,69 @@
             train_ref.at[:, pl.ds(p * 2 * chunk, 2 * chunk)], stored.at[p], load_sem.at[p]
         )
 
-    def z_copy(src, b, p, send, target):
-        return pltpu.make_async_remote_copy(
-            src_ref=src, dst_ref=held.at[b, p, :, w], send_sem=send.at[b, p],
+    def pick(p, first, second):
+        @pl.when(p < shared)
+        def _():
+            first()
+
+        @pl.when(p >= shared)
+        def _():
+            second()
+
+    def z_copy(src, b, p, which, send, target):
+        return pltpu.make_async_remote_copy(
+            src_ref=src, dst_ref=held.at[b, p, which, w], send_sem=send.at[b, p],
             recv_sem=z_recv.at[b, p], device_id=target, device_id_type=MESH,
         )
 
     def own_z(p, send, target):
-        return z_copy(own_ref.at[p], zz, p, send, target)
-
-    def pass_z(b, p, send, target):
-        return z_copy(held.at[b, p, :, w], b, p, send, target)
+        pick(
+            p,
+            lambda: z_copy(own_ref.at[p, side], zz, p, side, send, target).start(),
+            lambda: z_copy(own_ref.at[p], zz, p, slice(None), send, target).start(),
+        )
+
+    def pass_z(b, p, send, target, act):
+        pick(
+            p,
+            lambda: act(z_copy(held.at[b, p, side, w], b, p, side, send, target)),
+            lambda: act(z_copy(held.at[b, p, :, w], b, p, slice(None), send, target)),
+        )
+
+    def begin(copy):
+        copy.start()
+
+    def landed(copy):
+        copy.wait_recv()
+
+    def left_here(copy):
+        copy.wait_send()
 
     def y_copy(src, b, p):
         return pltpu.make_async_remote_copy(
             src_ref=src, dst_ref=held.at[b, p, side, w], send_sem=y_send.at[b, p],
             recv_sem=y_recv.at[b, p], device_id=across_y, device_id_type=MESH,
         )
+
+    def y_whole(b, p, column):
+        slot = held.at[b, p, :, column]
+        return pltpu.make_async_remote_copy(
+            src_ref=slot, dst_ref=slot, send_sem=y_send.at[b, p],
+            recv_sem=y_recv.at[b, p], device_id=across_y, device_id_type=MESH,
+        )
+
+    def twin_copy(b, p, which):
+        slot = held.at[b, p, which, w]
+        return pltpu.make_async_remote_copy(
+            src_ref=slot, dst_ref=slot, send_sem=twin_send.at[b, p],
+            recv_sem=twin_recv.at[b, p], device_id=across_x, device_id_type=MESH,
+        )
+
+    def whole_over_y(t, p):
+        return jnp.logical_and(jnp.asarray(t) != 0, jnp.asarray(p) == pairs - 1)
+
+    def from_twin(t, p):
+        return jnp.logical_and(jnp.asarray(t) != 0, jnp.asarray(p) < shared)
 
     def y_arrival(b, p):
         slot = held.at[b, p, side, 1 - w]
@@ -115,11 +163,11 @@
     def _(p):
         @pl.when(has_right)
         def _():
-            own_z(p, zr_send, right).start()
+            own_z(p, zr_send, right)
 
         @pl.when(has_left)
         def _():
-            own_z(p, zl_send, left).start()
+            own_z(p, zl_send, left)
 
         y_copy(own_ref.at[p, side], zz, p).start()
 
@@ -155,26 +203,49 @@
         @pl.when(t > 0)
         def _():
             if from_left:
-                pass_z(b, p, zr_send, left).wait_recv()
+                pass_z(b, p, zr_send, left, landed)
 
                 @pl.when(has_right)
                 def _():
-                    pass_z(b, p, zr_send, right).start()
+                    pass_z(b, p, zr_send, right, begin)
             else:
-                pass_z(b, p, zl_send, right).wait_recv()
+                pass_z(b, p, zl_send, right, landed)
 
                 @pl.when(has_left)
                 def _():
-                    pass_z(b, p, zl_send, left).start()
-
-            y_copy(held.at[b, p, side, w], b, p).start()
+                    pass_z(b, p, zl_send, left, begin)
+
+            @pl.when(p < shared)
+            def _():
+                twin_copy(b, p, side).start()
+
+            @pl.when(p < pairs - 1)
+            def _():
+                y_copy(held.at[b, p, side, w], b, p).start()
+
+            @pl.when(p == pairs - 1)
+            def _():
+                y_whole(b, p, w).start()
 
     def relay_x(b, t, p, from_left):
-        y_arrival(b, p).wait_recv()
-        x_copy(b, p, side).start()
+        @pl.when(jnp.logical_not(whole_over_y(t, p)))
+        def _():
+            y_arrival(b, p).wait_recv()
+            x_copy(b, p, side).start()
 
     def multiply(b, t, p, from_left):
-        x_copy(b, p, 1 - side).wait_recv()
+        @pl.when(from_twin(t, p))
+        def _():
+            twin_copy(b, p, 1 - side).wait_recv()
+
+        @pl.when(whole_over_y(t, p))
+        def _():
+            y_whole(b, p, 1 - w).wait_recv()
+
+        @pl.when(jnp.logical_not(whole_over_y(t, p)))
+        def _():
+            x_copy(b, p, 1 - side).wait_recv()
+
         for part in range(2):
             value = None
             for h in range(2):
@@ -247,14 +318,26 @@
 
         @pl.when(jnp.logical_and(has_right, b <= zz))
         def _():
-            pass_z(b, p, zr_send, right).wait_send()
+            pass_z(b, p, zr_send, right, left_here)
 
         @pl.when(jnp.logical_and(has_left, b >= zz))
         def _():
-            pass_z(b, p, zl_send, left).wait_send()
-
-        y_copy(held.at[b, p, side, w], b, p).wait_send()
-        x_copy(b, p, side).wait_send()
+            pass_z(b, p, zl_send, left, left_here)
+
+        t = b - zz
+
+        @pl.when(from_twin(t, p))
+        def _():
+            twin_copy(b, p, side).wait_send()
+
+        @pl.when(whole_over_y(t, p))
+        def _():
+            y_whole(b, p, w).wait_send()
+
+        @pl.when(jnp.logical_not(whole_over_y(t, p)))
+        def _():
+            y_copy(held.at[b, p, side, w], b, p).wait_send()
+            x_copy(b, p, side).wait_send()
 
         @pl.when(p == 0)
         def _():
@@ -267,7 +350,7 @@
     examples = train.shape[0]
     line = devices // 2
     dma = pltpu.SemaphoreType.DMA
-    grid_sems = [dma((line, pairs)) for _ in range(7)]
+    grid_sems = [dma((line, pairs)) for _ in range(9)]
     return pl.pallas_call(
         functools.partial(score_kernel, line),
         out_shape=jax.ShapeDtypeStruct((line, 2 * rows, examples // 2), jnp.float32),

time: 72.6 us -> 72.4 us (level)
  no operation moved by 1% of the time
where the time goes in v3:
time: 72.4 us; the launch traced here: 72.1 us
  Pallas kernels  53.7 us (74%)
  matrix products  8.9 us (12%)
  local copies, waits for them, and re-layouts  6.63 us (9%)
  other arithmetic  2.14 us (3%)
  between operations  0.73 us (1%)
    pallas_call x1, Pallas kernels, scores_of(): pl.pallas_call(functools.partial(score_kernel, line), out_shape=jax.Shape...  53.7 us
    dot_general x1, matrix products, precondition(): jnp.einsum('nlik,lkm->nlim', expanded, basis_a, precision=highest)  3.14 us
    unnamed x5, local copies, waits for them, and re-layouts  2.27 us
    dot_general x1, matrix products, precondition(): jnp.einsum('nljm,lpm->nljp', scaled, basis_a, precision=highest)  2.13 us
    another operation x1, local copies, waits for them, and re-layouts  2.07 us
    dot_general x1, matrix products, precondition(): jnp.einsum('lij,nlim->nljm', basis_s, half_turn, precision=highest)  1.85 us
    dot_general x1, matrix products, precondition(): jnp.einsum('lij,nljp->nlip', basis_s, turned_back, precision=highest)  1.79 us

profile of v3, /device:TPU:1, one launch (start us, length us, event | category | flops | bytes accessed | tf_op | source)
XLA Modules:
  0.0 72.1 jit_solution(10328643748905452402)
XLA Ops:
  0.0 0.0 copy-start
  0.0 1.4 %reduce_sum.9 = f32[]{:T(128)} reduce(f32[1,64,64]{2,1,0:T(8,128)} %param.9, f32[]{:T(128)} %constant.6.clone.1), dimensions={0,1,2}, to_apply=%region_0.0 | reduce | flops 4095 | bytes 16392 | tf_op jit(solution)/shard_map/reduce_sum | solution.py:24
  2.0 0.8 %add_bitcast_fusion = f32[64,64]{1,0:T(8,128)S(1)} fusion(f32[1,64,64]{2,1,0:T(8,128)} %param.9, f32[]{:T(128)S(6)} %mul.4), kind=kLoop, calls=%fused_computation.13 | loop fusion | flops 4096 | bytes 32772 | tf_op jit(solution)/shard_map/div | solution.py:25
  2.8 0.1 copy.10
  2.9 0.0 copy-start.1
  2.9 2.1 %reshape.52 = bf16[64,64,64]{2,1,0:T(8,128)(2,1)S(1)} reshape(bf16[64,1,4096]{2,0,1:T(8,128)(2,1)} %param.6) | data formatting | bytes 1048576 | tf_op jit(solution)/shard_map/reshape.1
  5.0 0.0 copy-done
  5.0 3.1 %fusion.8 = f32[64,64,64]{2,0,1:T(8,128)S(1)} fusion(bf16[64,64,64]{2,1,0:T(8,128)(2,1)S(1)} %reshape.52, f32[1,64,64]{2,1,0:T(8,128)S(1)} %copy-done), kind=kOutput, calls=%fused_computation.9 | convolution fusion | flops 201326592 | bytes 1589248 | tf_op jit(solution)/shard_map/nlik,lkm->nlim/dot_general | solution.py:22
  8.1 0.0 copy-done.1
  8.1 1.8 %fusion.3 = f32[64,64,64]{2,1,0:T(8,128)S(1)} fusion(f32[64,64,64]{2,0,1:T(8,128)S(1)} %fusion.8, f32[1,64,64]{2,1,0:T(8,128)S(1)} %copy-done.1), kind=kOutput, calls=%fused_computation.3 | convolution fusion | flops 201326592 | bytes 2113536 | tf_op jit(solution)/shard_map/lij,nlim->nljm/dot_general | solution.py:23
  10.0 2.1 %fusion.1 = f32[64,64,64]{1,2,0:T(8,128)S(1)} fusion(f32[64,64,64]{2,1,0:T(8,128)S(1)} %fusion.3, f32[64,64]{0,1:T(8,128)S(1)} %copy.10, f32[1,64,64]{2,1,0:T(8,128)S(1)} %copy-done), kind=kOutput, calls=%fused_computation.2 | convolution fusion | flops 201588736 | bytes 2129920 | tf_op jit(solution)/shard_map/nljm,lpm->nljp/dot_general | solution.py:26
  12.1 1.8 %fusion.5 = bf16[64,1,64,64]{2,3,0,1:T(8,128)(2,1)S(1)} fusion(f32[64,64,64]{1,2,0:T(8,128)S(1)} %fusion.1, f32[1,64,64]{2,1,0:T(8,128)S(1)} %copy-done.1), kind=kOutput, calls=%fused_computation.6 | convolution fusion | flops 201588736 | bytes 1589248 | tf_op jit(solution)/shard_map/lij,nljp->nlip/dot_general | solution.py:27
  13.9 0.7 copy.11
  14.6 0.6 convert_element_type.19
  15.2 0.9 %copy.12 = bf16[8,64,512]{2,1,0:T(8,128)(2,1)} copy(bf16[8,64,512]{2,0,1:T(8,128)(2,1)S(1)} %bitcast.51) | data formatting | bytes 1048576 | tf_op jit(solution)/shard_map/transpose | solution.py:386
  16.1 53.7 %shard_map.64 = f32[4,128,512]{2,1,0:T(8,128)} custom-call(bf16[4,2,64,512]{3,2,1,0:T(8,128)(2,1)} %bitcast.52, s32[1,1024]{1,0:T(1,128)} %ids_ref.1, bf16[1024,4096]{1,0:T(8,128)(2,1)} %bitcast.49), custom_call_target="tpu_custom_call" | custom-call | tf_op jit(solution)/shard_map/pallas_call | solution.py:354
  69.8 2.3 %copy.16 = f32[512,512]{1,0:T(8,128)} copy(f32[512,512]{1,0:T(8,128)} %bitcast.50) | data formatting | bytes 2097152
Async XLA Ops:
  0.0 5.0 %copy-start = (f32[1,64,64]{2,1,0:T(8,128)S(1)}, f32[1,64,64]{2,1,0:T(8,128)}, u32[]{:S(2)}) copy-start(f32[1,64,64]{2,1,0:T(8,128)} %param.8) | copy-start | bytes 49156
  2.9 5.2 %copy-start.1 = (f32[1,64,64]{2,1,0:T(8,128)S(1)}, f32[1,64,64]{2,1,0:T(8,128)}, u32[]{:S(2)}) copy-start(f32[1,64,64]{2,1,0:T(8,128)} %param.7) | copy-start | bytes 49156

commit v4 on v3

--- a/solution.py
+++ b/solution.py
@@ -30,7 +30,7 @@
 
 def score_kernel(
     line, own_ref, ids_ref, train_ref, out_ref,
-    stored, hot, perm, held, acc, arrived,
+    stored, hot, held, acc, arrived,
     load_sem, own_sem, z_recv, zr_send, zl_send, y_recv, y_send, x_recv, x_send, twin_recv, twin_send,
     c_recv, c_send,
 ):
@@ -233,7 +233,36 @@
             y_arrival(b, p).wait_recv()
             x_copy(b, p, side).start()
 
+    def reorder(b):
+        pieces = []
+        for source in range(2):
+            rest = acc[b, source]
+            terms = []
+            for _ in range(3):
+                term = rest.astype(jnp.bfloat16)
+                terms.append(term)
+                rest = rest - term.astype(jnp.float32)
+            pieces.append(jnp.concatenate(terms, axis=0))
+        ordered = []
+        for part in range(2):
+            value = None
+            for source in range(2):
+                term = lax.dot_general(
+                    pieces[source],
+                    hot[part * half:(part + 1) * half, source * half:(source + 1) * half],
+                    (((1,), (1,)), ((), ())), preferred_element_type=jnp.float32,
+                )
+                value = term if value is None else value + term
+            block = 2 * rows
+            ordered.append(value[:block] + value[block:2 * block] + value[2 * block:])
+        for part in range(2):
+            acc[b, part] = ordered[part]
+
     def multiply(b, t, p, from_left):
+        @pl.when(t == 0)
+        def _():
+            load(p).wait()
+
         @pl.when(from_twin(t, p))
         def _():
             twin_copy(b, p, 1 - side).wait_recv()
@@ -251,7 +280,7 @@
             for h in range(2):
                 term = lax.dot_general(
                     held[b, p, h].reshape(2 * rows, chunk),
-                    perm[p, h, part * half:(part + 1) * half, :],
+                    stored[p, part * half:(part + 1) * half, h * chunk:(h + 1) * chunk],
                     (((1,), (1,)), ((), ())), preferred_element_type=jnp.float32,
                 )
                 value = term if value is None else value + term
@@ -266,6 +295,7 @@
 
         @pl.when(p == pairs - 1)
         def _():
+            reorder(b)
             c_copy(b).start()
 
     def finish(b, t, p, from_left):
@@ -279,7 +309,7 @@
         relay_x(zz, 0, p, True)
 
     def reached(s):
-        ready = jnp.minimum(2 * (s - pairs + 1), s + pairs - 1)
+        ready = jnp.minimum(3 * jnp.maximum(s, 0) // 2, s + pairs - 1)
         return jnp.minimum(jnp.maximum(ready, 0), line * pairs)
 
     @pl.loop(0, (line + 1) * pairs)
@@ -289,20 +319,6 @@
         @pl.when(s > 0)
         def _():
             both(s + pairs - 1, relay_x)
-
-        @pl.when(s < pairs)
-        def _():
-            load(s).wait()
-
-            @pl.loop(0, 4)
-            def _(part):
-                quarter = examples // 4
-                picked = pl.ds(part * quarter, quarter)
-                for h in range(2):
-                    perm[s, h, picked, :] = jnp.dot(
-                        hot[picked, :], stored[s, :, h * chunk:(h + 1) * chunk],
-                        preferred_element_type=jnp.float32,
-                    ).astype(jnp.bfloat16)
 
         @pl.loop(reached(s - 1), reached(s))
         def _(m):
@@ -363,7 +379,6 @@
         scratch_shapes=[
             pltpu.VMEM((pairs, examples, 2 * chunk), jnp.bfloat16),
             pltpu.VMEM((examples, examples), jnp.bfloat16),
-            pltpu.VMEM((pairs, 2, examples, chunk), jnp.bfloat16),
             pltpu.VMEM((line, pairs, 2, 2, rows, chunk), jnp.bfloat16),
             pltpu.VMEM((line, 2, 2 * rows, examples // 2), jnp.float32),
             pltpu.VMEM((line, 2 * rows, examples // 2), jnp.float32),

time: 72.4 us -> 73.1 us (level)
  no operation moved by 1% of the time
where the time goes in v4:
time: 73.1 us; the launch traced here: 72.7 us
  Pallas kernels  54.3 us (74%)
  matrix products  8.9 us (12%)
  local copies, waits for them, and re-layouts  6.63 us (9%)
  other arithmetic  2.14 us (3%)
    pallas_call x1, Pallas kernels, scores_of(): pl.pallas_call(functools.partial(score_kernel, line), out_shape=jax.Shape...  54.3 us
    dot_general x1, matrix products, precondition(): jnp.einsum('nlik,lkm->nlim', expanded, basis_a, precision=highest)  3.14 us
    unnamed x5, local copies, waits for them, and re-layouts  2.27 us
    dot_general x1, matrix products, precondition(): jnp.einsum('nljm,lpm->nljp', scaled, basis_a, precision=highest)  2.13 us
    another operation x1, local copies, waits for them, and re-layouts  2.07 us
    dot_general x1, matrix products, precondition(): jnp.einsum('lij,nlim->nljm', basis_s, half_turn, precision=highest)  1.85 us
    dot_general x1, matrix products, precondition(): jnp.einsum('lij,nljp->nlip', basis_s, turned_back, precision=highest)  1.79 us

profile of v4, /device:TPU:1, one launch (start us, length us, event | category | flops | bytes accessed | tf_op | source)
XLA Modules:
  0.0 72.7 jit_solution(7840802015000121457)
XLA Ops:
  0.0 0.0 copy-start
  0.0 1.4 %reduce_sum.9 = f32[]{:T(128)} reduce(f32[1,64,64]{2,1,0:T(8,128)} %param.9, f32[]{:T(128)} %constant.6.clone.1), dimensions={0,1,2}, to_apply=%region_0.0 | reduce | flops 4095 | bytes 16392 | tf_op jit(solution)/shard_map/reduce_sum | solution.py:24
  2.0 0.8 %add_bitcast_fusion = f32[64,64]{1,0:T(8,128)S(1)} fusion(f32[1,64,64]{2,1,0:T(8,128)} %param.9, f32[]{:T(128)S(6)} %mul.4), kind=kLoop, calls=%fused_computation.13 | loop fusion | flops 4096 | bytes 32772 | tf_op jit(solution)/shard_map/div | solution.py:25
  2.8 0.1 copy.10
  2.9 0.0 copy-start.1
  2.9 2.1 %reshape.52 = bf16[64,64,64]{2,1,0:T(8,128)(2,1)S(1)} reshape(bf16[64,1,4096]{2,0,1:T(8,128)(2,1)} %param.6) | data formatting | bytes 1048576 | tf_op jit(solution)/shard_map/reshape.1
  5.0 0.0 copy-done
  5.0 3.1 %fusion.8 = f32[64,64,64]{2,0,1:T(8,128)S(1)} fusion(bf16[64,64,64]{2,1,0:T(8,128)(2,1)S(1)} %reshape.52, f32[1,64,64]{2,1,0:T(8,128)S(1)} %copy-done), kind=kOutput, calls=%fused_computation.9 | convolution fusion | flops 201326592 | bytes 1589248 | tf_op jit(solution)/shard_map/nlik,lkm->nlim/dot_general | solution.py:22
  8.1 0.0 copy-done.1
  8.1 1.8 %fusion.3 = f32[64,64,64]{2,1,0:T(8,128)S(1)} fusion(f32[64,64,64]{2,0,1:T(8,128)S(1)} %fusion.8, f32[1,64,64]{2,1,0:T(8,128)S(1)} %copy-done.1), kind=kOutput, calls=%fused_computation.3 | convolution fusion | flops 201326592 | bytes 2113536 | tf_op jit(solution)/shard_map/lij,nlim->nljm/dot_general | solution.py:23
  10.0 2.1 %fusion.1 = f32[64,64,64]{1,2,0:T(8,128)S(1)} fusion(f32[64,64,64]{2,1,0:T(8,128)S(1)} %fusion.3, f32[64,64]{0,1:T(8,128)S(1)} %copy.10, f32[1,64,64]{2,1,0:T(8,128)S(1)} %copy-done), kind=kOutput, calls=%fused_computation.2 | convolution fusion | flops 201588736 | bytes 2129920 | tf_op jit(solution)/shard_map/nljm,lpm->nljp/dot_general | solution.py:26
  12.1 1.8 %fusion.5 = bf16[64,1,64,64]{2,3,0,1:T(8,128)(2,1)S(1)} fusion(f32[64,64,64]{1,2,0:T(8,128)S(1)} %fusion.1, f32[1,64,64]{2,1,0:T(8,128)S(1)} %copy-done.1), kind=kOutput, calls=%fused_computation.6 | convolution fusion | flops 201588736 | bytes 1589248 | tf_op jit(solution)/shard_map/lij,nljp->nlip/dot_general | solution.py:27
  13.9 0.7 copy.11
  14.6 0.6 convert_element_type.19
  15.2 0.9 %copy.12 = bf16[8,64,512]{2,1,0:T(8,128)(2,1)} copy(bf16[8,64,512]{2,0,1:T(8,128)(2,1)S(1)} %bitcast.51) | data formatting | bytes 1048576 | tf_op jit(solution)/shard_map/transpose | solution.py:401
  16.1 54.3 %shard_map.64 = f32[4,128,512]{2,1,0:T(8,128)} custom-call(bf16[4,2,64,512]{3,2,1,0:T(8,128)(2,1)} %bitcast.52, s32[1,1024]{1,0:T(1,128)} %ids_ref.1, bf16[1024,4096]{1,0:T(8,128)(2,1)} %bitcast.49), custom_call_target="tpu_custom_call" | custom-call | tf_op jit(solution)/shard_map/pallas_call | solution.py:370
  70.5 2.3 %copy.16 = f32[512,512]{1,0:T(8,128)} copy(f32[512,512]{1,0:T(8,128)} %bitcast.50) | data formatting | bytes 2097152
Async XLA Ops:
  0.0 5.0 %copy-start = (f32[1,64,64]{2,1,0:T(8,128)S(1)}, f32[1,64,64]{2,1,0:T(8,128)}, u32[]{:S(2)}) copy-start(f32[1,64,64]{2,1,0:T(8,128)} %param.8) | copy-start | bytes 49156
  2.9 5.2 %copy-start.1 = (f32[1,64,64]{2,1,0:T(8,128)S(1)}, f32[1,64,64]{2,1,0:T(8,128)}, u32[]{:S(2)}) copy-start(f32[1,64,64]{2,1,0:T(8,128)} %param.7) | copy-start | bytes 49156

commit v5 on v3

--- a/solution.py
+++ b/solution.py
@@ -17,14 +17,14 @@
     number_rows = grads.shape[0]
     layer_count = grads.shape[1]
     rank = basis_s.shape[-1]
-    highest = lax.Precision.HIGHEST
+    high = lax.Precision.HIGH
     expanded = grads.astype(jnp.float32).reshape(number_rows, layer_count, rank, rank)
-    half_turn = jnp.einsum("nlik,lkm->nlim", expanded, basis_a, precision=highest)
-    rotated = jnp.einsum("lij,nlim->nljm", basis_s, half_turn, precision=highest)
+    half_turn = jnp.einsum("nlik,lkm->nlim", expanded, basis_a, precision=high)
+    rotated = jnp.einsum("lij,nlim->nljm", basis_s, half_turn, precision=high)
     damping = damp_ratio * jnp.mean(eigvals, axis=(1, 2), keepdims=True)
     scaled = rotated / (eigvals + damping)[None]
-    turned_back = jnp.einsum("nljm,lpm->nljp", scaled, basis_a, precision=highest)
-    restored = jnp.einsum("lij,nljp->nlip", basis_s, turned_back, precision=highest)
+    turned_back = jnp.einsum("nljm,lpm->nljp", scaled, basis_a, precision=high)
+    restored = jnp.einsum("lij,nljp->nlip", basis_s, turned_back, precision=high)
     return restored.reshape(number_rows, layer_count, rank * rank).astype(jnp.bfloat16)
 
 

time: 72.4 us -> 68.7 us (0.949)
  matrix products: 8.9 us -> 5.1 us
    dot_general x4, matrix products: 8.9 us -> 5.1 us  [the longest x1 2.15 us: precondition(): half_turn = jnp.einsum('nlik,lkm->nlim', expanded, basis_a, precision=high)]
where the time goes in v5:
time: 68.7 us; the launch traced here: 68.3 us
  Pallas kernels  53.7 us (78%)
  local copies, waits for them, and re-layouts  6.63 us (10%)
  matrix products  5.1 us (7%)
  other arithmetic  2.14 us (3%)
  between operations  0.73 us (1%)
    pallas_call x1, Pallas kernels, scores_of(): pl.pallas_call(functools.partial(score_kernel, line), out_shape=jax.Shape...  53.7 us
    unnamed x5, local copies, waits for them, and re-layouts  2.27 us
    dot_general x1, matrix products, precondition(): half_turn = jnp.einsum('nlik,lkm->nlim', expanded, basis_a, precision=high)  2.15 us
    another operation x1, local copies, waits for them, and re-layouts  2.07 us
    reduce_sum x1, other arithmetic, precondition(): damping = damp_ratio * jnp.mean(eigvals, axis=(1, 2), keepdims=True)  1.38 us

profile of v5, /device:TPU:1, one launch (start us, length us, event | category | flops | bytes accessed | tf_op | source)
XLA Modules:
  0.0 68.3 jit_solution(11871206492707159020)
XLA Ops:
  0.0 0.0 copy-start
  0.0 1.4 %reduce_sum.9 = f32[]{:T(128)} reduce(f32[1,64,64]{2,1,0:T(8,128)} %param.9, f32[]{:T(128)} %constant.6.clone.1), dimensions={0,1,2}, to_apply=%region_0.0 | reduce | flops 4095 | bytes 16392 | tf_op jit(solution)/shard_map/reduce_sum | solution.py:24
  2.0 0.8 %add_bitcast_fusion = f32[64,64]{1,0:T(8,128)S(1)} fusion(f32[1,64,64]{2,1,0:T(8,128)} %param.9, f32[]{:T(128)S(6)} %mul.4), kind=kLoop, calls=%fused_computation.13 | loop fusion | flops 4096 | bytes 32772 | tf_op jit(solution)/shard_map/div | solution.py:25
  2.8 0.1 copy.10
  2.9 0.0 copy-start.1
  2.9 2.1 %reshape.52 = bf16[64,64,64]{2,1,0:T(8,128)(2,1)S(1)} reshape(bf16[64,1,4096]{2,0,1:T(8,128)(2,1)} %param.6) | data formatting | bytes 1048576 | tf_op jit(solution)/shard_map/reshape.1
  5.0 0.0 copy-done
  5.0 2.1 %fusion.8 = f32[64,64,64]{2,0,1:T(8,128)S(1)} fusion(bf16[64,64,64]{2,1,0:T(8,128)(2,1)S(1)} %reshape.52, f32[1,64,64]{2,1,0:T(8,128)S(1)} %copy-done), kind=kOutput, calls=%fused_computation.9 | convolution fusion | flops 100663296 | bytes 1589248 | tf_op jit(solution)/shard_map/nlik,lkm->nlim/dot_general | solution.py:22
  7.1 0.0 copy-done.1
  7.1 1.0 %fusion.3 = f32[64,64,64]{2,1,0:T(8,128)S(1)} fusion(f32[64,64,64]{2,0,1:T(8,128)S(1)} %fusion.8, f32[1,64,64]{2,1,0:T(8,128)S(1)} %copy-done.1), kind=kOutput, calls=%fused_computation.3 | convolution fusion | flops 100663296 | bytes 2113536 | tf_op jit(solution)/shard_map/lij,nlim->nljm/dot_general | solution.py:23
  8.1 1.0 %fusion.1 = f32[64,64,64]{1,2,0:T(8,128)S(1)} fusion(f32[64,64,64]{2,1,0:T(8,128)S(1)} %fusion.3, f32[64,64]{0,1:T(8,128)S(1)} %copy.10, f32[1,64,64]{2,1,0:T(8,128)S(1)} %copy-done), kind=kOutput, calls=%fused_computation.2 | convolution fusion | flops 100925440 | bytes 2129920 | tf_op jit(solution)/shard_map/nljm,lpm->nljp/dot_general | solution.py:26
  9.1 1.0 %fusion.5 = bf16[64,1,64,64]{2,3,0,1:T(8,128)(2,1)S(1)} fusion(f32[64,64,64]{1,2,0:T(8,128)S(1)} %fusion.1, f32[1,64,64]{2,1,0:T(8,128)S(1)} %copy-done.1), kind=kOutput, calls=%fused_computation.6 | convolution fusion | flops 100925440 | bytes 1589248 | tf_op jit(solution)/shard_map/lij,nljp->nlip/dot_general | solution.py:27
  10.1 0.7 copy.11
  10.8 0.6 convert_element_type.19
  11.4 0.9 %copy.12 = bf16[8,64,512]{2,1,0:T(8,128)(2,1)} copy(bf16[8,64,512]{2,0,1:T(8,128)(2,1)S(1)} %bitcast.51) | data formatting | bytes 1048576 | tf_op jit(solution)/shard_map/transpose | solution.py:386
  12.3 53.7 %shard_map.64 = f32[4,128,512]{2,1,0:T(8,128)} custom-call(bf16[4,2,64,512]{3,2,1,0:T(8,128)(2,1)} %bitcast.52, s32[1,1024]{1,0:T(1,128)} %ids_ref.1, bf16[1024,4096]{1,0:T(8,128)(2,1)} %bitcast.49), custom_call_target="tpu_custom_call" | custom-call | tf_op jit(solution)/shard_map/pallas_call | solution.py:354
  66.1 2.3 %copy.16 = f32[512,512]{1,0:T(8,128)} copy(f32[512,512]{1,0:T(8,128)} %bitcast.50) | data formatting | bytes 2097152
Async XLA Ops:
  0.0 5.0 %copy-start = (f32[1,64,64]{2,1,0:T(8,128)S(1)}, f32[1,64,64]{2,1,0:T(8,128)}, u32[]{:S(2)}) copy-start(f32[1,64,64]{2,1,0:T(8,128)} %param.8) | copy-start | bytes 49156
  2.9 4.2 %copy-start.1 = (f32[1,64,64]{2,1,0:T(8,128)S(1)}, f32[1,64,64]{2,1,0:T(8,128)}, u32[]{:S(2)}) copy-start(f32[1,64,64]{2,1,0:T(8,128)} %param.7) | copy-start | bytes 49156
